TPU v7x, 256 devices: a whole 4x4x8 slice. The times are simulated.
256 devices in a mesh: ctx: 32 (over z_hi, x, core), head: 8 (over z_lo, y).
Axes of the slice: x: 4, y: 4, z: 8 (z_hi: 4, z_lo: 2; z = z_hi * 2 + z_lo), core: 2. Of those that a mesh axis runs over, the one named last changes fastest.
Arguments:
- activations: bfloat16 [4096, 8192], P('ctx', 'head'), may hold values from -6 to 6
- query_base: bfloat16 [4096, 8192], P('ctx', 'head'), may hold values from -150 to 150
- key_rows: bfloat16 [4096, 1024], P('ctx', 'head'), may hold values from -4 to 4
- values: bfloat16 [4096, 1024], P('ctx', 'head'), may hold values from -6 to 6
- out_cotangent: bfloat16 [4096, 8192], P('ctx', 'head'), may hold values from -0.3984375 to 0.3984375
- adapter_a: bfloat16 [8192, 16], P('head'), may hold values from -0.0625 to 0.0625
- adapter_b: bfloat16 [16, 8192], P(None, 'head'), may hold values from -1.5 to 1.5
- tangent_a: bfloat16 [8192, 16], P('head'), may hold values from -0.0625 to 0.0625
- tangent_b: bfloat16 [16, 8192], P(None, 'head'), may hold values from -1.5 to 1.5
- segment_ids: int32 [4096], P('ctx'), may hold values from 0 to 7, as said below
- doc_starts: int32 [8], replicated, may hold values from 0 to 4095, as said below
Outputs:
- hvp_a: float32 [8192, 16], P('head')
- hvp_b: float32 [16, 8192], P(None, 'head')
Inputs may be any that keep to these rules, and one draw needn't show every extreme that they name: `segment_ids`: segment numbers never fall along the tokens, and every number from 0 to 7 occurs. doc_starts[s] is the first position of segment s; starts rise strictly, doc_starts[0] is 0, every later start is 2560 or more, and the last is 4095.
All inputs are finite; a program needn't handle non-finite values.
Results may differ from a plain program's by a relative error of at most 0.0091.
Values may be sent and summed in bfloat16 or wider, within the bound.
A program may use at most 64 MiB of HBM per device.

v0:
```python
import functools, math
import jax, jax.numpy as jnp
from jax import lax
from jax.experimental import pallas as pl
from jax.experimental.pallas import tpu as pltpu

HS = 128
TILE = 2
ONES = 16
NT = (((1,), (1,)), ((), ()))
TN = (((0,), (0,)), ((), ()))
NN = (((1,), (0,)), ((), ()))
f32, bf16 = jnp.float32, jnp.bfloat16
SCALE = 1.0 / math.sqrt(HS)
CEXP = SCALE * math.log2(math.e)


def mm(a, b, dims=NN):
    return lax.dot_general(a, b, dims, preferred_element_type=f32)


def split2(x):
    hi = x.astype(bf16)
    return hi, (x - hi.astype(f32)).astype(bf16)


def split3(x):
    hi = x.astype(bf16)
    r = x - hi.astype(f32)
    mid = r.astype(bf16)
    return hi, mid, (r - mid.astype(f32)).astype(bf16)


def make_queries(low_t, qb_ref, cot_ref, b, tb, q_s, t_s, g_s):
    l3 = split3(low_t[0:16, :])
    lt3 = split3(low_t[16:32, :])
    q_all = mm(jnp.concatenate(l3, 0), jnp.concatenate([b, b, b], 0), TN) + qb_ref[...].astype(f32)
    t_all = mm(jnp.concatenate(lt3 + l3, 0), jnp.concatenate([b, b, b, tb, tb, tb], 0), TN)
    for h in range(q_s.shape[0]):
        cols = slice(h * HS, (h + 1) * HS)
        q_s[h] = q_all[:, cols].astype(bf16)
        t_s[h] = t_all[:, cols].astype(bf16)
        g_s[h] = cot_ref[:, cols]


def pick(ref, ti):
    v = ref[pl.ds(ti * TILE, TILE)]
    return v.reshape(TILE * v.shape[1], HS)


def weights(s, mc, kblk, vblk, t2, g2):
    e = jnp.exp2(s * CEXP - mc)
    t = mm(kblk, t2, NT)
    p = mm(vblk, g2, NT)
    w1 = e * p
    w2 = e * t
    w3 = w1 * t
    return jnp.concatenate([e.astype(bf16), w1.astype(bf16), w2.astype(bf16), w3.astype(bf16)], axis=1)


def transpose_keys(kblk):
    return jnp.concatenate([kblk.T, jnp.ones((ONES, kblk.shape[0]), bf16)], axis=0)


def own_tile(ti, first, base, starts, kblk, vblk, kt, q_s, t_s, g_s, s_own, acc_o, m_o):
    rows = starts.shape[1]
    n_keys = kblk.shape[0]
    pos = base + lax.broadcasted_iota(jnp.int32, (1, rows), 1)
    starts2 = jnp.concatenate([starts] * TILE, axis=1)
    pos2 = jnp.concatenate([pos] * TILE, axis=1)
    s = mm(kblk[...], pick(q_s, ti), NT)
    kp = first + lax.broadcasted_iota(jnp.int32, s.shape, 0)
    s = jnp.where((kp >= starts2) & (kp <= pos2), s, -1e30)
    s_own[...] = s
    m = jnp.max(jnp.max(s.reshape(n_keys // 8, 8, s.shape[1]), axis=0), axis=0, keepdims=True)
    m_o[ti] = jnp.broadcast_to(m, m_o.shape[1:])
    w = weights(s_own[...], m * CEXP, kblk[...], vblk[...], pick(t_s, ti), pick(g_s, ti))
    acc_o[ti] = mm(kt[...], w)


def attend_kernel(kb_len, own_fn, starts_ref, m_ref, q_s, t_s, g_s, k_ref, v_ref, acc_in, acc, s_buf, kt, m_new):
    lanes = TILE * starts_ref.shape[1]
    starts = starts_ref[...]
    start_last = jnp.max(starts)
    lo = jnp.min(starts) // kb_len
    hi = own_fn()
    starts2 = jnp.concatenate([starts] * TILE, axis=1)

    def build(kb, c):
        off = pl.multiple_of(kb * kb_len, kb_len)
        kt[:, pl.ds(off, kb_len)] = transpose_keys(k_ref[pl.ds(off, kb_len), :])
        return c

    lax.fori_loop(lo, hi, build, 0)

    def one_tile(ti, carry):
        q2, t2, g2 = pick(q_s, ti), pick(t_s, ti), pick(g_s, ti)
        m_old = m_ref[ti]
        m_new[...] = m_old

        def pass1(kb, c):
            off = pl.multiple_of(kb * kb_len, kb_len)

            def keep(s):
                s_buf[pl.ds(off, kb_len), :] = s
                m_new[...] = jnp.maximum(m_new[...], jnp.max(s.reshape(kb_len // 8, 8, lanes), axis=0))

            @pl.when(off < start_last)
            def _():
                s = mm(k_ref[pl.ds(off, kb_len), :], q2, NT)
                kp = off + lax.broadcasted_iota(jnp.int32, (kb_len, lanes), 0)
                keep(jnp.where(kp >= starts2, s, -1e30))

            @pl.when(off >= start_last)
            def _():
                keep(mm(k_ref[pl.ds(off, kb_len), :], q2, NT))
            return c

        lax.fori_loop(lo, hi, pass1, 0)
        m = jnp.max(m_new[...], axis=0, keepdims=True)
        mc = m * CEXP
        factor = jnp.exp2(m_old[0:1] * CEXP - mc)
        acc[ti] = acc[ti] * jnp.concatenate([factor] * 4, axis=1)

        def pass2(kb, c):
            off = pl.multiple_of(kb * kb_len, kb_len)
            w = weights(s_buf[pl.ds(off, kb_len), :], mc, k_ref[pl.ds(off, kb_len), :], v_ref[pl.ds(off, kb_len), :], t2, g2)
            acc[ti] += mm(kt[:, pl.ds(off, kb_len)], w)
            return c

        lax.fori_loop(lo, hi, pass2, 0)
        return carry

    lax.fori_loop(0, jnp.where(lo < hi, acc.shape[0], 0), one_tile, 0)


def attend(starts, m_o, q_s, t_s, g_s, k, v, acc, own_fn, kb_len):
    total = k.shape[0]
    lanes = TILE * starts.shape[1]
    vm = pl.BlockSpec(memory_space=pltpu.VMEM)
    return pl.pallas_call(
        functools.partial(attend_kernel, kb_len, own_fn),
        out_shape=jax.ShapeDtypeStruct(acc.shape, f32),
        in_specs=[vm] * 8,
        out_specs=vm,
        scratch_shapes=[
            pltpu.VMEM((total, lanes), f32),
            pltpu.VMEM((HS + ONES, total), bf16),
            pltpu.VMEM((8, lanes), f32),
        ],
        input_output_aliases={7: 0},
        compiler_params=pltpu.CompilerParams(vmem_limit_bytes=32 << 20),
        name="attend",
    )(starts, m_o, q_s, t_s, g_s, k, v, acc)


def close_tiles(acc_ref, low_t, b, tb, zp, bp):
    rows = low_t.shape[1]
    lanes = TILE * rows
    l3 = split2(low_t[0:16, :])
    lt3 = split2(low_t[16:32, :])
    llt = jnp.concatenate([lt3[0], lt3[0], lt3[1], l3[0], l3[0], l3[1]], axis=1)
    zz = jnp.zeros((16, rows), f32)
    for ti in range(acc_ref.shape[0]):
        a = acc_ref[ti]
        k0, k1, k2, k3 = (a[0:HS, n * lanes:(n + 1) * lanes] for n in range(4))
        l, aa, bb, cc = (a[HS:HS + 1, n * lanes:(n + 1) * lanes] for n in range(4))
        inv = 1.0 / l
        delta = aa * inv
        mt = bb * inv * SCALE
        dd = cc * inv * SCALE - mt * delta
        f = SCALE * inv
        grad = (k1 - delta * k0) * f
        gdot = (SCALE * (k3 - delta * k2) - mt * k1 + (mt * delta - dd) * k0) * f
        gh, gl = split2(grad)
        dh, dl = split2(gdot)
        for j in range(TILE):
            cols = slice((ti * TILE + j) * HS, (ti * TILE + j + 1) * HS)
            bj, tbj = b[:, cols], tb[:, cols]
            ln = slice(j * rows, (j + 1) * rows)
            zz += mm(jnp.concatenate([bj, bj, tbj, tbj], 1),
                     jnp.concatenate([dh[:, ln], dl[:, ln], gh[:, ln], gl[:, ln]], 0))
            r = jnp.concatenate([gh[:, ln], gl[:, ln], gh[:, ln], dh[:, ln], dl[:, ln], dh[:, ln]], axis=1)
            bp[ti * TILE + j] = mm(llt, r, NT)
    zp[...] = zz


from jax.sharding import PartitionSpec as P

MESH = pl.DeviceIdType.MESH
NX, NC, NZ = 4, 2, 4
GROUP = NX * NC


def place():
    ctx = lax.axis_index("ctx")
    return ctx, ctx // GROUP, (ctx // NC) % NX, ctx % NC


def at(z, x, core):
    return (z % NZ) * GROUP + (x % NX) * NC + core


def greet(ctx_peers, head_peers):
    barrier = pltpu.get_barrier_semaphore()
    for p in ctx_peers:
        pl.semaphore_signal(barrier, inc=1, device_id={"ctx": p}, device_id_type=MESH)
    for p in head_peers:
        pl.semaphore_signal(barrier, inc=1, device_id={"head": p}, device_id_type=MESH)
    return lambda: pl.semaphore_wait(barrier, len(ctx_peers) + len(head_peers))


def gather_kernel(n_head, k_ref, v_ref, x_ref, a_ref, ta_ref, qb_ref, cot_ref, b_ref, tb_ref, seg_ref, docs_ref,
                  kall, vall, low_ref, x_o, b_o, tb_o, starts_ref, q_s, t_s, g_s, acc_o, m_o,
                  qb_o, cot_o, s_own, kt, a_s, parts, mine, seg_s, docs_s, rk, rv, rl, ss, sl, loc):
    ctx, z, x, core = place()
    head = lax.axis_index("head")
    rows = k_ref.shape[0]
    heads = [lax.rem(head + d, n_head) for d in range(1, n_head)]
    twin = at(z, x, 1 - core)
    sides = [at(z, x + dx, core) for dx in (1, 3, 2)]
    ahead = [at(z + dz, x, core) for dz in range(NZ)]
    ready = greet(sides + ahead[1:] + [twin], heads)

    def cut(ref, j):
        return ref.at[pl.ds(pl.multiple_of(j * rows, rows), rows), :]

    pairs = [(x_ref, x_o), (a_ref, a_s.at[0:16]), (ta_ref, a_s.at[16:32]), (k_ref, cut(kall, ctx)), (v_ref, cut(vall, ctx)),
             (seg_ref, seg_s), (docs_ref, docs_s), (qb_ref, qb_o), (cot_ref, cot_o), (b_ref, b_o), (tb_ref, tb_o)]
    loads = [pltpu.make_async_copy(s, d, loc.at[i]) for i, (s, d) in enumerate(pairs)]
    for c in loads:
        c.start()
    for c in loads[:3]:
        c.wait()
    part = mm(a_s[...], x_o[...], NT)
    mine[...] = part
    parts[pl.ds(head, 1)] = part[None]
    ready()
    lows = []
    for i, p in enumerate(heads):
        c = pltpu.make_async_remote_copy(
            src_ref=mine, dst_ref=parts.at[head], send_sem=sl.at[i], recv_sem=rl.at[head],
            device_id={"head": p}, device_id_type=MESH)
        c.start()
        lows.append(c)

    sends = []
    count = [0]

    def push(kv, j, tos, cond=None, src=None):
        ref, sem = kv
        for to in tos:
            n = count[0]
            count[0] += 1

            def make(n=n, to=to):
                return pltpu.make_async_remote_copy(
                    src_ref=cut(ref, j) if src is None else src, dst_ref=cut(ref, j), send_sem=ss.at[n],
                    recv_sem=sem.at[j], device_id={"ctx": to}, device_id_type=MESH)

            make().start()
            sends.append((cond, make))

    K, V = (kall, rk), (vall, rv)

    def arrive(kv, j):
        ref, sem = kv
        pltpu.make_async_remote_copy(
            src_ref=cut(ref, j), dst_ref=cut(ref, j), send_sem=ss.at[0], recv_sem=sem.at[j],
            device_id={"ctx": twin}, device_id_type=MESH).wait_recv()

    def when(cond, f):
        if cond is None:
            f()
        else:
            pl.when(cond)(f)

    has = {0: None, 1: z >= 1, 2: z >= 2, 3: z >= 3}
    to1, to2, to3 = z <= 2, z <= 1, z == 0
    spot = [[at(z + NZ - d, x + dx, core) for dx in range(NX)] for d in range(NZ)]
    other = [[at(z + NZ - d, xx, 1 - core) for xx in range(NX)] for d in range(NZ)]

    for kv, src in ((K, k_ref), (V, v_ref)):
        when(to2, lambda: push(kv, ctx, [ahead[2]], to2, src))
        when(to1, lambda: push(kv, ctx, [ahead[1]], to1, src))
        push(kv, ctx, sides + [twin], None, src)
    for kv, src in ((K, k_ref), (V, v_ref)):
        when(to3, lambda: push(kv, ctx, [ahead[3]], to3, src))

    for c in loads[3:]:
        c.wait()
    seg = seg_s[...]
    starts = jnp.zeros(seg.shape, jnp.int32)
    for d in range(docs_s.shape[0]):
        starts = jnp.where(seg == d, docs_s[d], starts)
    starts_ref[...] = starts

    def row(d):
        for kv in (K, V):
            for dx in (1, 3, 2):
                arrive(kv, spot[d][dx])
                push(kv, spot[d][dx], [twin], has[d])

    def column(d):
        for kv in (K, V):
            arrive(kv, spot[d][0])
            push(kv, spot[d][0], sides + [twin], has[d])

    def low_sum():
        for i, p in enumerate(heads):
            pltpu.make_async_remote_copy(
                src_ref=mine, dst_ref=parts.at[p], send_sem=sl.at[i], recv_sem=rl.at[p],
                device_id={"head": p}, device_id_type=MESH).wait_recv()
        low_ref[...] = jnp.sum(parts[...], axis=0)

    def twins(d):
        for xx in range(NX):
            j = other[d][xx]
            arrive(K, j)
            arrive(V, j)

    when(has[1], lambda: column(1))
    row(0)
    low_sum()
    twins(0)
    span = GROUP * rows
    first = pl.multiple_of(z * span, span)
    kblk, vblk = kall.at[pl.ds(first, span), :], vall.at[pl.ds(first, span), :]
    kt[...] = transpose_keys(kblk[...])
    make_queries(low_ref[...], qb_o, cot_o, b_o[...], tb_o[...], q_s, t_s, g_s)

    def own(ti):
        own_tile(ti, first, ctx * rows, starts, kblk, vblk, kt, q_s, t_s, g_s, s_own, acc_o, m_o)

    own(0)
    when(has[2], lambda: column(2))
    when(has[3], lambda: column(3))
    own(1)
    when(has[1], lambda: row(1))
    own(2)
    own(3)
    when(has[2], lambda: row(2))
    when(has[3], lambda: row(3))
    for d in range(1, NZ):
        when(has[d], lambda: twins(d))
    groups = {}
    for cond, make in sends:
        groups.setdefault(id(cond), (cond, []))[1].append(make)

    def drain(makes):
        for make in makes:
            make().wait_send()

    for cond, makes in groups.values():
        when(cond, lambda: drain(makes))
    for c in lows:
        c.wait_send()


def gather(k, v, x, a_t, ta_t, qb, cot, b, tb, seg, docs, n_ctx, n_head):
    rows, width = k.shape
    vm = pl.BlockSpec(memory_space=pltpu.VMEM)
    hb = pl.BlockSpec(memory_space=pltpu.HBM)
    dma = pltpu.SemaphoreType.DMA
    like = jax.ShapeDtypeStruct
    args = (k, v, x, a_t, ta_t, qb, cot, b, tb, seg.reshape(1, rows), docs)
    n_q = qb.shape[1] // HS
    stack = like((n_q, rows, HS), bf16)
    lanes = TILE * rows
    return pl.pallas_call(
        functools.partial(gather_kernel, n_head),
        out_shape=(like((n_ctx * rows, width), bf16), like((n_ctx * rows, width), bf16), like((32, rows), f32),
                   like(x.shape, bf16), like(b.shape, bf16), like(tb.shape, bf16), like((1, rows), jnp.int32),
                   stack, stack, stack, like((n_q // TILE, HS + ONES, 4 * lanes), f32), like((n_q // TILE, 8, lanes), f32)),
        in_specs=[hb] * 11,
        out_specs=(vm,) * 12,
        scratch_shapes=[
            pltpu.VMEM(qb.shape, bf16),
            pltpu.VMEM(cot.shape, bf16),
            pltpu.VMEM((GROUP * rows, lanes), f32),
            pltpu.VMEM((HS + ONES, GROUP * rows), bf16),
            pltpu.VMEM((32, x.shape[1]), bf16),
            pltpu.VMEM((n_head, 32, rows), f32),
            pltpu.VMEM((32, rows), f32),
            pltpu.VMEM((1, rows), jnp.int32),
            pltpu.SMEM(docs.shape, jnp.int32),
            dma((n_ctx,)), dma((n_ctx,)), dma((n_head,)), dma((96,)), dma((n_head,)), dma((11,)),
        ],
        compiler_params=pltpu.CompilerParams(collective_id=0, has_side_effects=True, vmem_limit_bytes=20 << 20),
        name="gather",
    )(*(pltpu.with_memory_space_constraint(r, pltpu.HBM) for r in args))


def reduce_kernel(n_head, acc_ref, low_ref, b_ref, tb_ref, x_ref, oa_ref, ob_ref, zp_ref, zbuf, sa, sb, ra, rb, ca, cb, ta, tb,
                  rz, zs, rsa, rsb, ssa, ssb, rca, rcb, sca, scb, rga, rgb, sga, sgb):
    ctx, z, x, core = place()
    u = lax.rem(ctx, GROUP)
    head = lax.axis_index("head")
    heads = [lax.rem(head + d, n_head) for d in range(1, n_head)]
    mates = [lax.rem(u + d, GROUP) for d in range(1, GROUP)]
    cols = [lax.rem(z + d, NZ) for d in range(1, NZ)]
    ready = greet([z * GROUP + m for m in mates] + [c * GROUP + u for c in cols], heads)
    close_tiles(acc_ref, low_ref[...], b_ref[...], tb_ref[...], zp_ref, sb)
    zbuf[pl.ds(head, 1)] = zp_ref[...][None]
    ready()
    sends = []

    def copy(src, dst, ssem, rsem, dev):
        return pltpu.make_async_remote_copy(src_ref=src, dst_ref=dst, send_sem=ssem, recv_sem=rsem,
                                            device_id=dev, device_id_type=MESH)

    def start(c):
        c.start()
        sends.append(c)

    for i, p in enumerate(heads):
        start(copy(zp_ref, zbuf.at[head], zs.at[i], rz.at[head], {"head": p}))

    def scatter(s, r, ssem, rsem):
        for i, m in enumerate(mates):
            start(copy(s.at[m], r.at[u], ssem.at[i], rsem.at[u], {"ctx": z * GROUP + m}))
        r[pl.ds(u, 1)] = s[pl.ds(u, 1)]

    def across(r, c, s, rsem, ssem2, rsem2):
        for i, m in enumerate(mates):
            copy(r.at[m], r.at[m], ssem2.at[0], rsem.at[m], {"ctx": z * GROUP + m}).wait_recv()
        part = jnp.sum(r[...], axis=0)
        s[...] = part
        c[pl.ds(z, 1)] = part[None]
        for i, q in enumerate(cols):
            start(copy(s, c.at[z], ssem2.at[i], rsem2.at[z], {"ctx": q * GROUP + u}))

    def spread(c, t, o, ssem, rsem, ssem2, rsem2):
        for i, q in enumerate(cols):
            copy(t.at[q], c.at[q], ssem.at[0], rsem.at[q], {"ctx": q * GROUP + u}).wait_recv()
        t[pl.ds(u, 1)] = jnp.sum(c[...], axis=0)[None]
        for i, m in enumerate(mates):
            start(copy(t.at[u], t.at[u], ssem2.at[i], rsem2.at[u], {"ctx": z * GROUP + m}))

    def collect(t, o, ssem, rsem):
        for m in mates:
            copy(t.at[m], t.at[m], ssem.at[0], rsem.at[m], {"ctx": z * GROUP + m}).wait_recv()
        for i in range(GROUP):
            o[:, i * HS:(i + 1) * HS] = t[i]

    scatter(sb, rb, ssb, rsb)
    for i, p in enumerate(heads):
        copy(zp_ref, zbuf.at[p], zs.at[0], rz.at[p], {"head": p}).wait_recv()
    zsum = jnp.sum(zbuf[...], axis=0)
    ap = mm(jnp.concatenate(split3(zsum), 0), x_ref[...])
    ap = ap[0:16] + ap[16:32] + ap[32:48]
    for i in range(GROUP):
        sa[i] = ap[:, i * HS:(i + 1) * HS]
    scatter(sa, ra, ssa, rsa)
    across(rb, cb, sb_part(sb), rsb, scb, rcb)
    across(ra, ca, sb_part(sa), rsa, sca, rca)
    spread(cb, tb, ob_ref, scb, rcb, sgb, rgb)
    spread(ca, ta, oa_ref, sca, rca, sga, rga)
    collect(tb, ob_ref, sgb, rgb)
    collect(ta, oa_ref, sga, rga)
    for c in sends:
        c.wait_send()


def sb_part(s):
    return s.at[GROUP]


def reduce(acc, low_t, b, tb, x, n_head):
    width = b.shape[1]
    rows = low_t.shape[1]
    vm = pl.BlockSpec(memory_space=pltpu.VMEM)
    out = jax.ShapeDtypeStruct((16, width), f32)
    dma = pltpu.SemaphoreType.DMA
    return pl.pallas_call(
        functools.partial(reduce_kernel, n_head),
        out_shape=(out, out),
        in_specs=[vm] * 5,
        out_specs=(vm, vm),
        scratch_shapes=[
            pltpu.VMEM((16, rows), f32),
            pltpu.VMEM((n_head, 16, rows), f32),
            pltpu.VMEM((GROUP + 1, 16, HS), f32), pltpu.VMEM((GROUP + 1, 16, HS), f32),
            pltpu.VMEM((GROUP, 16, HS), f32), pltpu.VMEM((GROUP, 16, HS), f32),
            pltpu.VMEM((NZ, 16, HS), f32), pltpu.VMEM((NZ, 16, HS), f32),
            pltpu.VMEM((GROUP, 16, HS), f32), pltpu.VMEM((GROUP, 16, HS), f32),
            dma((n_head,)), dma((n_head,)),
            dma((GROUP,)), dma((GROUP,)), dma((GROUP,)), dma((GROUP,)),
            dma((NZ,)), dma((NZ,)), dma((NZ,)), dma((NZ,)),
            dma((GROUP,)), dma((GROUP,)), dma((GROUP,)), dma((GROUP,)),
        ],
        compiler_params=pltpu.CompilerParams(collective_id=1, has_side_effects=True, vmem_limit_bytes=6 << 20),
        name="reduce",
    )(acc, low_t, b, tb, x)


def finish_kernel(a_ref, b_ref, oa_ref, ob_ref, sem):
    copies = [pltpu.make_async_copy(a_ref, oa_ref, sem.at[0]), pltpu.make_async_copy(b_ref, ob_ref, sem.at[1])]
    for c in copies:
        c.start()
    for c in copies:
        c.wait()


def finish(a, b):
    vm = pl.BlockSpec(memory_space=pltpu.VMEM)
    hb = pl.BlockSpec(memory_space=pltpu.HBM)
    return pl.pallas_call(
        finish_kernel,
        out_shape=(jax.ShapeDtypeStruct(a.shape, f32), jax.ShapeDtypeStruct(b.shape, f32)),
        in_specs=[vm, vm],
        out_specs=(hb, hb),
        scratch_shapes=[pltpu.SemaphoreType.DMA((2,))],
        compiler_params=pltpu.CompilerParams(vmem_limit_bytes=1 << 20),
        name="finish",
    )(a, b)


def on_device(n_ctx, n_head, activations, query_base, key_rows, values, out_cotangent, adapter_a, adapter_b, tangent_a, tangent_b,
              segment_ids, doc_starts):
    rows = activations.shape[0]
    kall, vall, low_t, x, b, tb, starts, q_s, t_s, g_s, acc, m_o = gather(
        key_rows, values, activations, adapter_a.T, tangent_a.T, query_base, out_cotangent, adapter_b, tangent_b,
        segment_ids, doc_starts, n_ctx, n_head)
    acc = attend(starts, m_o, q_s, t_s, g_s, kall, vall, acc, lambda: lax.axis_index("ctx") // GROUP, GROUP * rows)
    oa, ob = finish(*reduce(acc, low_t, b, tb, x, n_head))
    return oa.T, ob


def solution(mesh):
    wide = P("ctx", "head")
    placed = (wide,) * 5 + (P("head", None), P(None, "head"), P("head", None), P(None, "head"), P("ctx"), P())
    return jax.shard_map(
        functools.partial(on_device, mesh.shape["ctx"], mesh.shape["head"]),
        mesh=mesh,
        in_specs=placed,
        out_specs=(P("head", None), P(None, "head")),
        check_vma=False,
    )
```

profile of v0, /device:TPU:1, one launch (start us, length us, event | category | flops | bytes accessed | tf_op | source)
XLA Modules:
  0.0 60.9 jit_solution(5527716410847003065)
XLA Ops:
  0.6 23.2 %gather.1 = (bf16[4096,128]{1,0:T(8,128)(2,1)S(1)}, bf16[4096,128]{1,0:T(8,128)(2,1)S(1)}, f32[32,128]{1,0:T(8,128)S(1)}, bf16[128,1024]{1,0:T(8,128)(2,1)S(1)},...) custom-call(bf16[128,128]{1,0:T(8,128)(2,1)} %k_ref.1, ...), custom_call_target="tpu_custom_call" | custom-call | tf_op jit(solution)/shard_map/gather/pallas_call | solution.py:370
  23.9 0.2 attend.1.acc_ref
  24.1 36.1 %reduce.1 = (f32[16,1024]{1,0:T(8,128)S(1)}, f32[16,1024]{1,0:T(8,128)S(1)}) custom-call(f32[4,144,1024]{2,1,0:T(8,128)S(1)} %attend.1.acc_ref, f32[32,128]{1,0:T(8,128)S(1)} %get-tuple-element.26.low_ref, bf16[16,1024]{1,0:T(8,128)(2,1)S(1)} %get-tuple-element.27.b_ref, bf16[16,1024]{1,0:T(8,128)(2,1)S(1)} %get-tuple-element.28.tb_ref, ...), custom_call_target="tpu_custom_call" | custom-call | tf_op jit(solution)/shard_map/reduce/pallas_call | solution.py:475
  60.2 0.7 %finish.1 = (f32[16,1024]{1,0:T(8,128)}, f32[16,1024]{1,0:T(8,128)}) custom-call(f32[16,1024]{1,0:T(8,128)S(1)} %get-tuple-element.30.a_ref, f32[16,1024]{1,0:T(8,128)S(1)} %get-tuple-element.31.b_ref), custom_call_target="tpu_custom_call" | custom-call | tf_op jit(solution)/shard_map/finish/pallas_call | solution.py:508
where the time goes:
time: 61 us; the launch traced here: 60.9 us
  Pallas kernels  60.3 us (99%)
  between operations  0.66 us (1%)
    pallas_call x1, Pallas kernels, reduce(): pl.pallas_call(functools.partial(reduce_kernel, n_head), out_shape=(out,...  36.1 us
    pallas_call x1, Pallas kernels, gather(): pl.pallas_call(functools.partial(gather_kernel, n_head), out_shape=(like(...  23.2 us

commit v1 on v0

--- a/solution.py
+++ b/solution.py
@@ -65,20 +65,38 @@
 def own_tile(ti, first, base, starts, kblk, vblk, kt, q_s, t_s, g_s, s_own, acc_o, m_o):
     rows = starts.shape[1]
     n_keys = kblk.shape[0]
+    lead = pl.ds(0, n_keys)
     pos = base + lax.broadcasted_iota(jnp.int32, (1, rows), 1)
     starts2 = jnp.concatenate([starts] * TILE, axis=1)
     pos2 = jnp.concatenate([pos] * TILE, axis=1)
     s = mm(kblk[...], pick(q_s, ti), NT)
     kp = first + lax.broadcasted_iota(jnp.int32, s.shape, 0)
     s = jnp.where((kp >= starts2) & (kp <= pos2), s, -1e30)
-    s_own[...] = s
+    s_own[lead, :] = s
     m = jnp.max(jnp.max(s.reshape(n_keys // 8, 8, s.shape[1]), axis=0), axis=0, keepdims=True)
     m_o[ti] = jnp.broadcast_to(m, m_o.shape[1:])
-    w = weights(s_own[...], m * CEXP, kblk[...], vblk[...], pick(t_s, ti), pick(g_s, ti))
-    acc_o[ti] = mm(kt[...], w)
-
-
-def attend_kernel(kb_len, own_fn, starts_ref, m_ref, q_s, t_s, g_s, k_ref, v_ref, acc_in, acc, s_buf, kt, m_new):
+    w = weights(s_own[lead, :], m * CEXP, kblk[...], vblk[...], pick(t_s, ti), pick(g_s, ti))
+    acc_o[ti] = mm(kt[:, lead], w)
+
+
+def prev_tile(ti, first, starts, kblk, vblk, kt, q_s, t_s, g_s, s_own, acc_i, acc_o, m_i, m_o):
+    n_keys = kblk.shape[0]
+    starts2 = jnp.concatenate([starts] * TILE, axis=1)
+    s = mm(kblk[...], pick(q_s, ti), NT)
+    kp = first + lax.broadcasted_iota(jnp.int32, s.shape, 0)
+    s = jnp.where(kp >= starts2, s, -1e30)
+    s_own[...] = s
+    m_old = m_i[ti][0:1]
+    m = jnp.max(jnp.max(s.reshape(n_keys // 8, 8, s.shape[1]), axis=0), axis=0, keepdims=True)
+    mc = jnp.maximum(m_old, m) * CEXP
+    if m_o is not None:
+        m_o[ti] = jnp.broadcast_to(jnp.maximum(m_old, m), m_o.shape[1:])
+    factor = jnp.exp2(m_old * CEXP - mc)
+    w = weights(s_own[...], mc, kblk[...], vblk[...], pick(t_s, ti), pick(g_s, ti))
+    acc_o[ti] = acc_i[ti] * jnp.concatenate([factor] * 4, axis=1) + mm(kt[...], w)
+
+
+def attend_kernel(kb_len, own_fn, starts_ref, q_s, t_s, g_s, k_ref, v_ref, m_in, acc_in, m_ref, acc, s_buf, kt, m_new):
     lanes = TILE * starts_ref.shape[1]
     starts = starts_ref[...]
     start_last = jnp.max(starts)
@@ -121,6 +139,7 @@
         mc = m * CEXP
         factor = jnp.exp2(m_old[0:1] * CEXP - mc)
         acc[ti] = acc[ti] * jnp.concatenate([factor] * 4, axis=1)
+        m_ref[ti] = jnp.broadcast_to(m, m_new.shape)
 
         def pass2(kb, c):
             off = pl.multiple_of(kb * kb_len, kb_len)
@@ -140,21 +159,21 @@
     vm = pl.BlockSpec(memory_space=pltpu.VMEM)
     return pl.pallas_call(
         functools.partial(attend_kernel, kb_len, own_fn),
-        out_shape=jax.ShapeDtypeStruct(acc.shape, f32),
+        out_shape=(jax.ShapeDtypeStruct(m_o.shape, f32), jax.ShapeDtypeStruct(acc.shape, f32)),
         in_specs=[vm] * 8,
-        out_specs=vm,
+        out_specs=(vm, vm),
         scratch_shapes=[
             pltpu.VMEM((total, lanes), f32),
             pltpu.VMEM((HS + ONES, total), bf16),
             pltpu.VMEM((8, lanes), f32),
         ],
-        input_output_aliases={7: 0},
+        input_output_aliases={6: 0, 7: 1},
         compiler_params=pltpu.CompilerParams(vmem_limit_bytes=32 << 20),
         name="attend",
-    )(starts, m_o, q_s, t_s, g_s, k, v, acc)
-
-
-def close_tiles(acc_ref, low_t, b, tb, zp, bp):
+    )(starts, q_s, t_s, g_s, k, v, m_o, acc)
+
+
+def close_tiles(acc_ref, accs, low_t, b, tb, zp, bp):
     rows = low_t.shape[1]
     lanes = TILE * rows
     l3 = split2(low_t[0:16, :])
@@ -162,7 +181,7 @@
     llt = jnp.concatenate([lt3[0], lt3[0], lt3[1], l3[0], l3[0], l3[1]], axis=1)
     zz = jnp.zeros((16, rows), f32)
     for ti in range(acc_ref.shape[0]):
-        a = acc_ref[ti]
+        a = acc_ref[ti] if ti < LATE else accs[ti - LATE]
         k0, k1, k2, k3 = (a[0:HS, n * lanes:(n + 1) * lanes] for n in range(4))
         l, aa, bb, cc = (a[HS:HS + 1, n * lanes:(n + 1) * lanes] for n in range(4))
         inv = 1.0 / l
@@ -188,6 +207,16 @@
 from jax.sharding import PartitionSpec as P
 
 MESH = pl.DeviceIdType.MESH
+LATE = 3
+
+
+class Shifted:
+    def __init__(self, ref, by):
+        self.ref, self.by = ref, by
+
+    def __setitem__(self, i, v):
+        self.ref[i - self.by] = v
+
 NX, NC, NZ = 4, 2, 4
 GROUP = NX * NC
 
@@ -220,7 +249,7 @@
     twin = at(z, x, 1 - core)
     sides = [at(z, x + dx, core) for dx in (1, 3, 2)]
     ahead = [at(z + dz, x, core) for dz in range(NZ)]
-    ready = greet(sides + ahead[1:] + [twin], heads)
+    ready = greet(sides + [ahead[1], ahead[3], twin], heads)
 
     def cut(ref, j):
         return ref.at[pl.ds(pl.multiple_of(j * rows, rows), rows), :]
@@ -276,12 +305,11 @@
             pl.when(cond)(f)
 
     has = {0: None, 1: z >= 1, 2: z >= 2, 3: z >= 3}
-    to1, to2, to3 = z <= 2, z <= 1, z == 0
+    to1, to3, both = z <= 2, z == 0, (z >= 1) & (z <= 2)
     spot = [[at(z + NZ - d, x + dx, core) for dx in range(NX)] for d in range(NZ)]
     other = [[at(z + NZ - d, xx, 1 - core) for xx in range(NX)] for d in range(NZ)]
 
     for kv, src in ((K, k_ref), (V, v_ref)):
-        when(to2, lambda: push(kv, ctx, [ahead[2]], to2, src))
         when(to1, lambda: push(kv, ctx, [ahead[1]], to1, src))
         push(kv, ctx, sides + [twin], None, src)
     for kv, src in ((K, k_ref), (V, v_ref)):
@@ -304,6 +332,8 @@
     def column(d):
         for kv in (K, V):
             arrive(kv, spot[d][0])
+            if d == 1:
+                when(both, lambda: push(kv, spot[d][0], [ahead[1]], both))
             push(kv, spot[d][0], sides + [twin], has[d])
 
     def low_sum():
@@ -322,26 +352,47 @@
     when(has[1], lambda: column(1))
     row(0)
     low_sum()
+    make_queries(low_ref[...], qb_o, cot_o, b_o[...], tb_o[...], q_s, t_s, g_s)
     twins(0)
     span = GROUP * rows
     first = pl.multiple_of(z * span, span)
     kblk, vblk = kall.at[pl.ds(first, span), :], vall.at[pl.ds(first, span), :]
     kt[...] = transpose_keys(kblk[...])
-    make_queries(low_ref[...], qb_o, cot_o, b_o[...], tb_o[...], q_s, t_s, g_s)
+
+    u = lax.rem(ctx, GROUP)
 
     def own(ti):
-        own_tile(ti, first, ctx * rows, starts, kblk, vblk, kt, q_s, t_s, g_s, s_own, acc_o, m_o)
+        for low_u, high_u in ((0, 4), (4, 6), (6, 8)):
+            @pl.when((u >= low_u) & (u < high_u))
+            def _():
+                n = high_u * rows
+                kb, vb = kall.at[pl.ds(first, n), :], vall.at[pl.ds(first, n), :]
+                own_tile(ti, first, ctx * rows, starts, kb, vb, kt, q_s, t_s, g_s, s_own, acc_o, m_o)
 
     own(0)
+    own(1)
     when(has[2], lambda: column(2))
     when(has[3], lambda: column(3))
-    own(1)
+    own(2)
     when(has[1], lambda: row(1))
-    own(2)
     own(3)
+    when(has[1], lambda: twins(1))
+    back = pl.multiple_of(jnp.maximum(z - 1, 0) * span, span)
+    kpre, vpre = kall.at[pl.ds(back, span), :], vall.at[pl.ds(back, span), :]
+
+    def older(lo, hi):
+        for ti in range(lo, hi):
+            prev_tile(ti, back, starts, kpre, vpre, kt, q_s, t_s, g_s, s_own, acc_o, acc_o, m_o, m_o)
+
+    def older_first():
+        kt[...] = transpose_keys(kpre[...])
+        older(0, 2)
+
+    when(has[1], older_first)
     when(has[2], lambda: row(2))
     when(has[3], lambda: row(3))
-    for d in range(1, NZ):
+    when(has[1], lambda: older(2, LATE))
+    for d in range(2, NZ):
         when(has[d], lambda: twins(d))
     groups = {}
     for cond, make in sends:
@@ -391,7 +442,8 @@
     )(*(pltpu.with_memory_space_constraint(r, pltpu.HBM) for r in args))
 
 
-def reduce_kernel(n_head, acc_ref, low_ref, b_ref, tb_ref, x_ref, oa_ref, ob_ref, zp_ref, zbuf, sa, sb, ra, rb, ca, cb, ta, tb,
+def reduce_kernel(n_head, acc_ref, m_ref, starts_ref, kall, vall, q_s, t_s, g_s, low_ref, b_ref, tb_ref, x_ref, oa_ref, ob_ref,
+                  accs, kt, s_own, zp_ref, zbuf, sa, sb, ra, rb, ca, cb, ta, tb,
                   rz, zs, rsa, rsb, ssa, ssb, rca, rcb, sca, scb, rga, rgb, sga, sgb):
     ctx, z, x, core = place()
     u = lax.rem(ctx, GROUP)
@@ -400,7 +452,19 @@
     mates = [lax.rem(u + d, GROUP) for d in range(1, GROUP)]
     cols = [lax.rem(z + d, NZ) for d in range(1, NZ)]
     ready = greet([z * GROUP + m for m in mates] + [c * GROUP + u for c in cols], heads)
-    close_tiles(acc_ref, low_ref[...], b_ref[...], tb_ref[...], zp_ref, sb)
+    accs[...] = acc_ref[LATE:]
+
+    @pl.when(z >= 1)
+    def _():
+        span = GROUP * x_ref.shape[0]
+        back = pl.multiple_of(jnp.maximum(z - 1, 0) * span, span)
+        kpre, vpre = kall.at[pl.ds(back, span), :], vall.at[pl.ds(back, span), :]
+        kt[...] = transpose_keys(kpre[...])
+        for ti in range(LATE, acc_ref.shape[0]):
+            prev_tile(ti, back, starts_ref[...], kpre, vpre, kt, q_s, t_s, g_s, s_own, acc_ref,
+                      Shifted(accs, LATE), m_ref, None)
+
+    close_tiles(acc_ref, accs, low_ref[...], b_ref[...], tb_ref[...], zp_ref, sb)
     zbuf[pl.ds(head, 1)] = zp_ref[...][None]
     ready()
     sends = []
@@ -466,7 +530,7 @@
     return s.at[GROUP]
 
 
-def reduce(acc, low_t, b, tb, x, n_head):
+def reduce(acc, m_o, starts, kall, vall, q_s, t_s, g_s, low_t, b, tb, x, n_head):
     width = b.shape[1]
     rows = low_t.shape[1]
     vm = pl.BlockSpec(memory_space=pltpu.VMEM)
@@ -475,9 +539,12 @@
     return pl.pallas_call(
         functools.partial(reduce_kernel, n_head),
         out_shape=(out, out),
-        in_specs=[vm] * 5,
+        in_specs=[vm] * 12,
         out_specs=(vm, vm),
         scratch_shapes=[
+            pltpu.VMEM((acc.shape[0] - LATE,) + acc.shape[1:], f32),
+            pltpu.VMEM((HS + ONES, GROUP * rows), bf16),
+            pltpu.VMEM((GROUP * rows, TILE * rows), f32),
             pltpu.VMEM((16, rows), f32),
             pltpu.VMEM((n_head, 16, rows), f32),
             pltpu.VMEM((GROUP + 1, 16, HS), f32), pltpu.VMEM((GROUP + 1, 16, HS), f32),
@@ -489,9 +556,9 @@
             dma((NZ,)), dma((NZ,)), dma((NZ,)), dma((NZ,)),
             dma((GROUP,)), dma((GROUP,)), dma((GROUP,)), dma((GROUP,)),
         ],
-        compiler_params=pltpu.CompilerParams(collective_id=1, has_side_effects=True, vmem_limit_bytes=6 << 20),
+        compiler_params=pltpu.CompilerParams(collective_id=1, has_side_effects=True, vmem_limit_bytes=12 << 20),
         name="reduce",
-    )(acc, low_t, b, tb, x)
+    )(acc, m_o, starts, kall, vall, q_s, t_s, g_s, low_t, b, tb, x)
 
 
 def finish_kernel(a_ref, b_ref, oa_ref, ob_ref, sem):
@@ -522,8 +589,8 @@
     kall, vall, low_t, x, b, tb, starts, q_s, t_s, g_s, acc, m_o = gather(
         key_rows, values, activations, adapter_a.T, tangent_a.T, query_base, out_cotangent, adapter_b, tangent_b,
         segment_ids, doc_starts, n_ctx, n_head)
-    acc = attend(starts, m_o, q_s, t_s, g_s, kall, vall, acc, lambda: lax.axis_index("ctx") // GROUP, GROUP * rows)
-    oa, ob = finish(*reduce(acc, low_t, b, tb, x, n_head))
+    m_o, acc = attend(starts, m_o, q_s, t_s, g_s, kall, vall, acc, lambda: jnp.maximum(lax.axis_index("ctx") // GROUP - 1, 0), GROUP * rows)
+    oa, ob = finish(*reduce(acc, m_o, starts, kall, vall, q_s, t_s, g_s, low_t, b, tb, x, n_head))
     return oa.T, ob
 
 

time: 61 us -> 55.1 us (0.903)
  Pallas kernels: 60.3 us -> 54.1 us
    pallas_call x1, Pallas kernels: 36.1 us -> 32.3 us  [reduce(): pl.pallas_call(functools.partial(reduce_kernel, n_head), out_shape=(out,...]
    pallas_call x1, Pallas kernels: 23.2 us -> 20.9 us  [gather(): pl.pallas_call(functools.partial(gather_kernel, n_head), out_shape=(like(...]
where the time goes in v1:
time: 55.1 us; the launch traced here: 55 us
  Pallas kernels  54.1 us (98%)
  between operations  0.82 us (1%)
    pallas_call x1, Pallas kernels, reduce(): pl.pallas_call(functools.partial(reduce_kernel, n_head), out_shape=(out,...  32.3 us
    pallas_call x1, Pallas kernels, gather(): pl.pallas_call(functools.partial(gather_kernel, n_head), out_shape=(like(...  20.9 us

profile of v1, /device:TPU:1, one launch (start us, length us, event | category | flops | bytes accessed | tf_op | source)
XLA Modules:
  0.0 55.0 jit_solution(7244096311433185417)
XLA Ops:
  0.6 20.9 %gather.1 = (bf16[4096,128]{1,0:T(8,128)(2,1)S(1)}, bf16[4096,128]{1,0:T(8,128)(2,1)S(1)}, f32[32,128]{1,0:T(8,128)S(1)}, bf16[128,1024]{1,0:T(8,128)(2,1)S(1)},...) custom-call(bf16[128,128]{1,0:T(8,128)(2,1)} %k_ref.1, ...), custom_call_target="tpu_custom_call" | custom-call | tf_op jit(solution)/shard_map/gather/pallas_call | solution.py:421
  21.6 0.2 attend.1
  21.8 32.3 %reduce.1 = (f32[16,1024]{1,0:T(8,128)S(1)}, f32[16,1024]{1,0:T(8,128)S(1)}) custom-call(f32[4,144,1024]{2,1,0:T(8,128)S(1)} %get-tuple-element.28.acc_ref, f32[4,8,256]{2,1,0:T(8,128)S(1)} %get-tuple-element.29.m_ref, s32[1,128]{1,0:T(1,128)S(1)} %get-tuple-element.20.starts_ref, bf16[4096,128]{1,0:T(8,128)(2,1)S(1)} %get-tuple-element.24.k_ref.kall, ...), custom_call_target="tpu_custom_call" | custom-call | tf_op jit(solution)/shard_map/reduce/pallas_call | solution.py:539
  54.1 0.7 %finish.1 = (f32[16,1024]{1,0:T(8,128)}, f32[16,1024]{1,0:T(8,128)}) custom-call(f32[16,1024]{1,0:T(8,128)S(1)} %get-tuple-element.34.a_ref, f32[16,1024]{1,0:T(8,128)S(1)} %get-tuple-element.35.b_ref), custom_call_target="tpu_custom_call" | custom-call | tf_op jit(solution)/shard_map/finish/pallas_call | solution.py:575
